TPU v7x, 1024 devices: a whole 8x8x8 slice. The times are simulated.
1024 devices in a mesh: expert: 8 (over z), fsdp: 8 (over y), tensor: 16 (over x, core).
Axes of the slice: x: 8, y: 8, z: 8, core: 2. Of those that a mesh axis runs over, the one named last changes fastest.
Arguments:
- tokens: bfloat16 [1024, 4096], P('expert', 'tensor'), may hold values from -6 to 6
- expert_ids: int32 [1024, 2], P('expert'), may hold values from 0 to 7, all different within a row; in each aligned block of 128 rows (0 to 127, 128 to 255, ...) at most 48 rows name the same one
- gate_probs: float32 [1024, 2], P('expert'), may hold values from 0.1 to 1
- w_gate: bfloat16 [8, 4096, 14336], P('expert', 'tensor', 'fsdp'), may hold values from -0.09375 to 0.09375
- w_up: bfloat16 [8, 4096, 14336], P('expert', 'tensor', 'fsdp'), may hold values from -0.09375 to 0.09375
- w_down: bfloat16 [8, 14336, 4096], P('expert', 'fsdp', 'tensor'), may hold values from -0.046875 to 0.046875
Outputs:
- mixed: bfloat16 [1024, 4096], P('expert', 'tensor')
Inputs may be any that keep to these rules, and one draw needn't show every extreme that they name: `expert_ids`: in each aligned block of 128 tokens no expert is named by more than 48 tokens, a bound that some block reaches; a token names two different experts.
All inputs are finite; a program needn't handle non-finite values.
Results may differ from a plain program's by a relative error of at most 0.0049.
Values may be sent and summed in bfloat16 or wider, within the bound.
A program may use at most 32 MiB of HBM per device.

v0:
```python
import jax
import jax.numpy as jnp
from jax import lax
from jax.sharding import PartitionSpec as P


def body(tokens, expert_ids, gate_probs, w_gate, w_up, w_down):
    tok_rows, feature_part = tokens.shape
    experts = lax.axis_size("expert")
    capacity = 3 * tok_rows // experts
    slot_rows = experts * capacity
    flat_ids = expert_ids.reshape(-1)
    onehot = (flat_ids[:, None] == jnp.arange(experts, dtype=jnp.int32)[None, :]).astype(jnp.int32)
    slot_rank = jnp.cumsum(onehot, axis=0) - onehot
    slot_index = jnp.sum(slot_rank * onehot, axis=1)
    target = flat_ids * capacity + slot_index
    dispatch_map = (jnp.arange(slot_rows, dtype=jnp.int32)[:, None] == target[None, :]).astype(
        jnp.bfloat16
    )
    doubled = jnp.repeat(tokens, expert_ids.shape[1], axis=0)
    outgoing = jnp.dot(dispatch_map, doubled, preferred_element_type=jnp.float32).astype(
        jnp.bfloat16
    )
    outgoing = outgoing.reshape(experts, capacity, feature_part)
    arrived = lax.all_to_all(outgoing, "expert", split_axis=0, concat_axis=0, tiled=True).reshape(
        slot_rows, feature_part
    )
    gate_matrix = w_gate[0]
    up_matrix = w_up[0]
    down_matrix = w_down[0]
    hidden_width = gate_matrix.shape[1]
    gate_term = jnp.dot(arrived, gate_matrix, preferred_element_type=jnp.float32)
    up_term = jnp.dot(arrived, up_matrix, preferred_element_type=jnp.float32)
    summed = lax.psum_scatter(
        jnp.concatenate([gate_term, up_term], axis=1), "tensor", scatter_dimension=0, tiled=True
    )
    hidden_share = (jax.nn.silu(summed[:, :hidden_width]) * summed[:, hidden_width:]).astype(
        jnp.bfloat16
    )
    partial_value = jnp.dot(
        lax.all_gather(hidden_share, "tensor", axis=0, tiled=True),
        down_matrix,
        preferred_element_type=jnp.float32,
    )
    expert_total = lax.psum(partial_value, "fsdp")
    returned = lax.all_to_all(
        expert_total.reshape(experts, capacity, -1),
        "expert",
        split_axis=0,
        concat_axis=0,
        tiled=True,
    )
    weigh_returned = returned.reshape(slot_rows, -1)
    picked = weigh_returned[target].reshape(tok_rows, expert_ids.shape[1], weigh_returned.shape[1])
    mixed = jnp.sum(picked * gate_probs[:, :, None], axis=1)
    return mixed.astype(jnp.bfloat16)


def solution(mesh):
    return jax.shard_map(
        body,
        mesh=mesh,
        in_specs=(
            P("expert", "tensor"),
            P("expert", None),
            P("expert", None),
            P("expert", "tensor", "fsdp"),
            P("expert", "tensor", "fsdp"),
            P("expert", "fsdp", "tensor"),
        ),
        out_specs=P("expert", "tensor"),
        check_vma=False,
    )
```

profile of v0, /device:TPU:2, one launch (start us, length us, event | category | flops | bytes accessed | tf_op | source)
XLA Modules:
  0.0 269.9 jit_solution(15985429875003125135)
XLA Ops:
  6.5 0.0 copy-start
  6.5 0.0 copy-start.1
  6.5 0.0 reduce-scatter.2.cloned.1.call-start
  6.5 0.9 copy.8
  7.5 0.1 eq.40
  7.6 0.1 reshape.75
  7.8 0.6 reduce-window.6
  8.3 0.2 slice_reduce_fusion
  8.6 0.1 fusion.9
  8.7 0.9 broadcast_in_dim.2
  9.6 0.1 reshape.77
  9.7 0.2 convolution_convert_fusion
  9.9 27.0 %all_to_all.10 = bf16[8,48,256]{2,1,0:T(8,128)(2,1)S(1)} all-to-all(bf16[8,48,256]{2,1,0:T(8,128)(2,1)S(1)} %bitcast.31), channel_id=1, replica_groups=mesh['expert'=8,'fsdp'=8,'tensor'=16] {'expert'}, dimensions={0} | all-to-all | bytes 393216 | tf_op jit(solution)/shard_map/all_to_all | solution.py:25
  36.9 0.0 copy-done
  36.9 0.5 fusion.2
  37.4 0.0 copy-done.1
  37.4 0.5 fusion.4
  37.9 3.0 %pad_maximum_fusion = f32[384,3584]{1,0:T(8,128)} fusion(f32[384,1792]{1,0:T(8,128)S(1)} %fusion.2, f32[384,1792]{1,0:T(8,128)S(1)} %fusion.4), kind=kLoop, calls=%fused_computation.1 | loop fusion | flops 1376256 | bytes 11010048 | tf_op jit(solution)/shard_map/concatenate | solution.py:35
  41.0 0.0 copy-start.2
  41.0 0.0 reduce-scatter.2.cloned.1.call-update
  41.0 0.0 copy-start.3
  41.0 0.0 copy-start.4
  41.0 0.0 all-gather.2.cloned.1.call-start
  41.1 63.3 %reduce-scatter.2.cloned.1.call-done = f32[24,3584]{1,0:T(8,128)} async-done(((f32[384,3584]{1,0:T(8,128)}), f32[24,3584]{1,0:T(8,128)}) %reduce-scatter.2.cloned.1.call-update) | async-done | bytes 344080 | tf_op jit(solution)/shard_map/reduce_scatter | solution.py:34
  104.4 1.7 fusion.7
  106.0 0.0 all-gather.2.cloned.1.call-update
  106.1 0.0 all-reduce.2.cloned.1.call-start
  106.1 48.6 %all-gather.2.cloned.1.call-done = bf16[384,1792]{1,0:T(8,128)(2,1)} async-done(((bf16[24,1792]{1,0:T(8,128)(2,1)}), bf16[384,1792]{1,0:T(8,128)(2,1)}) %all-gather.2.cloned.1.call-update) | async-done | bytes 1376272 | tf_op jit(solution)/shard_map/all_gather | solution.py:41
  154.7 0.0 copy-done.2
  154.7 2.6 fusion
  157.3 0.0 all-reduce.2.cloned.1.call-update
  157.4 83.9 %all-reduce.2.cloned.1.call-done = f32[8,48,256]{2,1,0:T(8,128)} async-done(((f32[8,48,256]{2,1,0:T(8,128)}), f32[8,48,256]{2,1,0:T(8,128)}) %all-reduce.2.cloned.1.call-update) | async-done | bytes 393232 | tf_op jit(solution)/shard_map/psum | solution.py:45
  241.2 8.1 %all-to-all-start.1 = ((f32[8,48,256]{2,1,0:T(8,128)}), f32[8,48,256]{2,1,0:T(8,128)S(1)}, u32[]{:S(2)}, u32[]{:S(2)}) async-start(f32[8,48,256]{2,1,0:T(8,128)} %all-reduce.2.cloned.1.call-done), calls=%async_computation.2 | async-start | bytes 786432 | tf_op jit(solution)/shard_map/all_to_all | solution.py:46
  249.3 0.0 copy-done.3
  249.3 0.1 copy.10
  249.5 0.1 mul.49
  249.6 0.0 copy-done.4
  249.6 0.1 copy.11
  249.7 11.5 %all-to-all-done.1 = f32[8,48,256]{2,1,0:T(8,128)S(1)} async-done(((f32[8,48,256]{2,1,0:T(8,128)}), f32[8,48,256]{2,1,0:T(8,128)S(1)}, u32[]{:S(2)}, u32[]{:S(2)}) %all-to-all-start.1) | async-done | bytes 393248 | tf_op jit(solution)/shard_map/all_to_all | solution.py:46
  261.2 1.0 gather_fusion
  262.2 0.1 reshape.82
  262.3 1.0 multiply_reduce_fusion
  (7 shorter events, 0.1 us)
Async XLA Ops:
  6.5 30.3 %copy-start = (bf16[1,256,1792]{2,1,0:T(8,128)(2,1)S(1)}, bf16[1,256,1792]{2,1,0:T(8,128)(2,1)}, u32[]{:S(2)}) copy-start(bf16[1,256,1792]{2,1,0:T(8,128)(2,1)} %param.10) | copy-start | bytes 2752516
  6.5 30.9 %copy-start.1 = (bf16[1,256,1792]{2,1,0:T(8,128)(2,1)S(1)}, bf16[1,256,1792]{2,1,0:T(8,128)(2,1)}, u32[]{:S(2)}) copy-start(bf16[1,256,1792]{2,1,0:T(8,128)(2,1)} %param.9) | copy-start | bytes 2752516
  6.5 97.8 %reduce-scatter.2.cloned.1.call-start = ((), (), s32[]{:S(2)}) async-start(), calls=%async_computation.3 | async-start | bytes 5849088 | tf_op jit(solution)/shard_map/reduce_scatter | solution.py:34
  41.0 113.7 %copy-start.2 = (bf16[1,1792,256]{2,1,0:T(8,128)(2,1)S(1)}, bf16[1,1792,256]{2,1,0:T(8,128)(2,1)}, u32[]{:S(2)}) copy-start(bf16[1,1792,256]{2,1,0:T(8,128)(2,1)} %param.11) | copy-start | bytes 2752516
  41.0 208.3 %copy-start.3 = (s32[128,2]{0,1:T(2,128)S(1)}, s32[128,2]{0,1:T(2,128)}, u32[]{:S(2)}) copy-start(s32[128,2]{0,1:T(2,128)} %param.7) | copy-start | bytes 3076
  41.0 208.6 %copy-start.4 = (f32[128,2]{0,1:T(2,128)S(1)}, f32[128,2]{0,1:T(2,128)}, u32[]{:S(2)}) copy-start(f32[128,2]{0,1:T(2,128)} %param.8) | copy-start | bytes 3076
  41.0 113.7 %all-gather.2.cloned.1.call-start = ((), (), s32[]{:S(2)}) async-start(), calls=%async_computation.4 | async-start | bytes 1462272 | tf_op jit(solution)/shard_map/all_gather | solution.py:41
  106.1 135.1 %all-reduce.2.cloned.1.call-start = ((), (), s32[]{:S(2)}) async-start(), calls=%async_computation.5 | async-start | bytes 786432 | tf_op jit(solution)/shard_map/psum | solution.py:45
  241.2 20.0 %all-to-all-start.1 = ((f32[8,48,256]{2,1,0:T(8,128)}), f32[8,48,256]{2,1,0:T(8,128)S(1)}, u32[]{:S(2)}, u32[]{:S(2)}) async-start(f32[8,48,256]{2,1,0:T(8,128)} %all-reduce.2.cloned.1.call-done), calls=%async_computation.2 | async-start | bytes 786432 | tf_op jit(solution)/shard_map/all_to_all | solution.py:46
Sparse Core Ops, SparseCore 0:
  41.1 63.1 reduce-scatter.1
  107.4 47.2 all-gather.1
  157.5 83.6 all-reduce.1
where the time goes:
time: 270 us
  waiting for transfers between devices  207 us (77%)
  blocking collectives  27 us (10%)
  between operations  13.2 us (5%)
  starting transfers between devices  8.2 us (3%)
  other arithmetic  6.51 us (2%)
  matrix products  3.91 us (1%)
  local copies, waits for them, and re-layouts  3.88 us (1%)
    psum x1, waiting for transfers between devices, body(): expert_total = lax.psum(partial_value, 'fsdp')  83.9 us
    reduce_scatter x1, waiting for transfers between devices, body(): lax.psum_scatter(jnp.concatenate([gate_term, up_term], axis=1), 'tensor',...  63.3 us
    all_gather x1, waiting for transfers between devices, body(): lax.all_gather(hidden_share, 'tensor', axis=0, tiled=True)  48.6 us
    all_to_all x1, blocking collectives, body(): lax.all_to_all(outgoing, 'expert', split_axis=0, concat_axis=0, tiled=True)  27 us
    all_to_all x1, waiting for transfers between devices, body(): lax.all_to_all(expert_total.reshape(experts, capacity, -1), 'expert', spl...  11.5 us
    all_to_all x1, starting transfers between devices, body(): lax.all_to_all(expert_total.reshape(experts, capacity, -1), 'expert', spl...  8.11 us
  transfers between devices with their start and end apart: 4, of which 4 were waited for; matrix products, arithmetic and copies ran while one was open for 0% of the time, Pallas kernels for 0%

commit v1 on v0

v1 whole, which is shorter than its diff:
```python
import functools

import jax
import jax.numpy as jnp
from jax import lax
from jax.experimental import pallas as pl
from jax.experimental.pallas import tpu as pltpu
from jax.sharding import PartitionSpec as P

MESH = pl.DeviceIdType.MESH
CH = 16
BF = jnp.bfloat16
F32 = jnp.float32


def block_order(n):
    order = [0]
    for d in range(1, n // 2 + 1):
        order.append(d)
        if d != n - d:
            order.append(n - d)
    return order


def kernel(
    cfg,
    tok_hbm, ids_hbm, prob_hbm, wg_hbm, wu_hbm, wd_hbm, out_ref,
    tok, ids, prob, wgu, wd, outg, comb, xs, part, sf, sb, sl, rf, rb, rl, hid, osb, ret, mix, yrecv, yown, res,
    ld_sem, w_ss, w_rs, d_ss, d_rs, f_ss, f_rs, r_ss, r_rs, a_ss, a_rs, h_ss, h_rs, o_ss, o_rs, y1_ss, y1_rs, y2_ss, y2_rs,
):
    ne, nf, nx, cap = cfg["ne"], cfg["nf"], cfg["nx"], cfg["cap"]
    half, lag = cfg["half"], cfg["lag"]
    order = block_order(ne)
    per = cap // CH
    groups = ne * per // nx
    fwd_n, bwd_n = nx // 2, nx - 1 - nx // 2
    tokens_n = tok.shape[0]
    feat = tok.shape[1]

    z, y, t = lax.axis_index("expert"), lax.axis_index("fsdp"), lax.axis_index("tensor")
    x, c = t // 2, t % 2
    other = 1 - c
    sgn = 1 - 2 * c
    partner = (z, y, x * 2 + other)

    def at_x(k):
        return (x + sgn * k + 2 * nx) % nx

    def dev_x(k):
        return (z, y, at_x(k) * 2 + c)

    def dev_z(k):
        return ((z + k + ne) % ne, y, t)

    def dev_y(k):
        return (z, (y + k + nf) % nf, t)

    def remote(src, dst, ss, rs, dev):
        return pltpu.make_async_remote_copy(
            src_ref=src, dst_ref=dst, send_sem=ss, recv_sem=rs, device_id=dev, device_id_type=MESH
        )

    sends = []

    mine = pl.ds(pl.multiple_of(c * half, 128), half)
    theirs = pl.ds(pl.multiple_of(other * half, 128), half)
    loads = [
        pltpu.make_async_copy(ids_hbm, ids, ld_sem.at[0]),
        pltpu.make_async_copy(prob_hbm, prob, ld_sem.at[1]),
        pltpu.make_async_copy(tok_hbm, tok, ld_sem.at[2]),
        pltpu.make_async_copy(wg_hbm.at[:, mine], wgu.at[c, :, 0:half], ld_sem.at[3]),
        pltpu.make_async_copy(wu_hbm.at[:, mine], wgu.at[c, :, half : 2 * half], ld_sem.at[4]),
        pltpu.make_async_copy(wd_hbm, wd, ld_sem.at[5]),
    ]
    for copy in loads:
        copy.start()

    barrier = pltpu.get_barrier_semaphore()
    peers = [partner]
    if nx > 1:
        peers.append(dev_x(1))
        if nx > 2:
            peers.append(dev_x(-1))
    peers += [dev_z(k) for k in range(1, ne)]
    peers += [dev_y(k) for k in range(1, nf)]
    for peer in peers:
        pl.semaphore_signal(barrier, inc=1, device_id=peer, device_id_type=MESH)

    loads[0].wait()
    loads[1].wait()
    expert_row = lax.broadcasted_iota(jnp.int32, (ne, tokens_n), 0)
    first = expert_row == ids[0:1, :]
    second = expert_row == ids[1:2, :]
    named = jnp.where(first, 1.0, 0.0) + jnp.where(second, 1.0, 0.0)
    weight = jnp.where(first, prob[0:1, :], 0.0) + jnp.where(second, prob[1:2, :], 0.0)
    earlier = jnp.where(
        lax.broadcasted_iota(jnp.int32, (tokens_n, tokens_n), 0)
        < lax.broadcasted_iota(jnp.int32, (tokens_n, tokens_n), 1),
        1.0,
        0.0,
    ).astype(BF)
    rank = jnp.dot(named.astype(BF), earlier, preferred_element_type=F32)
    rank = jnp.where(named > 0.5, rank, -1.0)
    slot_row = lax.broadcasted_iota(jnp.int32, (cap, tokens_n), 0).astype(F32)
    loads[2].wait()
    for e in range(ne):
        chosen = slot_row == rank[e : e + 1, :]
        rows = jnp.dot(jnp.where(chosen, 1.0, 0.0).astype(BF), tok[...], preferred_element_type=F32)
        outg[e] = rows.astype(BF).reshape(per, CH, feat)
        comb[e * cap : (e + 1) * cap, :] = jnp.where(chosen, weight[e : e + 1, :], 0.0)

    pl.semaphore_wait(barrier, len(peers))

    swaps = [
        remote(wg_hbm.at[:, theirs], wgu.at[c, :, 0:half], w_ss.at[0], w_rs.at[0], partner),
        remote(wu_hbm.at[:, theirs], wgu.at[c, :, half : 2 * half], w_ss.at[1], w_rs.at[1], partner),
    ]
    for copy in swaps:
        copy.start()
        sends.append(copy)

    xs[c, 0:per] = outg[z]
    dispatch = [None]
    for p in range(1, ne):
        copy = remote(
            outg.at[(z - order[p] + ne) % ne], xs.at[c, p * per : (p + 1) * per], d_ss.at[p], d_rs.at[p], dev_z(-order[p])
        )
        copy.start()
        dispatch.append(copy)
        sends.append(copy)

    handed = {}

    def hand(p):
        if p in handed:
            return
        if p > 0:
            dispatch[p].wait_recv()
        view = xs.at[c, p * per : (p + 1) * per]
        copy = remote(view, view, f_ss.at[p], f_rs.at[p], partner)
        copy.start()
        handed[p] = copy
        sends.append(copy)

    def blocks_of(g):
        return range(g * nx // per, ((g + 1) * nx - 1) // per + 1)

    taken = set()
    loaded = []

    def first_product(g):
        for p in blocks_of(g):
            hand(p)
        if not loaded:
            for copy in (loads[3], loads[4]):
                copy.wait()
            for copy in swaps:
                copy.wait_recv()
            loaded.append(1)
        for p in blocks_of(g):
            if p not in taken:
                handed[p].wait_recv()
                taken.add(p)
        a0 = xs[0, g * nx : (g + 1) * nx].reshape(nx * CH, feat)
        a1 = xs[1, g * nx : (g + 1) * nx].reshape(nx * CH, feat)
        tile = cfg["tile"]
        for n in range(2 * half // tile):
            cols = slice(n * tile, (n + 1) * tile)
            acc = jnp.dot(a0, wgu[0, :, cols], preferred_element_type=F32)
            acc += jnp.dot(a1, wgu[1, :, cols], preferred_element_type=F32)
            part[g * nx : (g + 1) * nx, :, cols] = acc.reshape(nx, CH, tile)

    reduce_f, reduce_b = {}, {}

    def reduce_step(g, k):
        if k < fwd_n:
            value = part[g * nx + at_x(fwd_n - k)]
            if k > 0:
                reduce_f[g, k - 1].wait_recv()
                value = value + rf[g, k - 1].astype(F32)
            i = g * (nx - 1) + k
            if k < fwd_n - 1:
                sf[g, k] = value.astype(BF)
                copy = remote(sf.at[g, k], rf.at[g, k], r_ss.at[i], r_rs.at[i], dev_x(1))
            else:
                sl[g] = value
                copy = remote(sl.at[g], rl.at[g], r_ss.at[i], r_rs.at[i], dev_x(1))
            copy.start()
            reduce_f[g, k] = copy
            sends.append(copy)
        if k < bwd_n:
            value = part[g * nx + at_x(-(bwd_n - k))]
            if k > 0:
                reduce_b[g, k - 1].wait_recv()
                value = value + rb[g, k - 1].astype(F32)
            sb[g, k] = value.astype(BF)
            i = g * (nx - 1) + fwd_n + k
            copy = remote(sb.at[g, k], rb.at[g, k], r_ss.at[i], r_rs.at[i], dev_x(-1))
            copy.start()
            reduce_b[g, k] = copy
            sends.append(copy)

    given = {}

    def give(g, owner, n):
        view = hid.at[c, g * nx + owner]
        i = g * nx + n
        copy = remote(view, view, h_ss.at[i], h_rs.at[i], partner)
        copy.start()
        given[g, n] = copy
        sends.append(copy)

    gather_f, gather_b = {}, {}
    gf_n, gb_n = bwd_n, fwd_n

    def finish(g):
        value = part[g * nx + x]
        if fwd_n:
            reduce_f[g, fwd_n - 1].wait_recv()
            value = value + rl[g]
        if bwd_n:
            reduce_b[g, bwd_n - 1].wait_recv()
            value = value + rb[g, bwd_n - 1].astype(F32)
        gate, up = value[:, :half], value[:, half:]
        hid[c, g * nx + x] = (gate / (1.0 + jnp.exp(-gate)) * up).astype(BF)
        gather_step(g, 0)

    def gather_step(g, k):
        if k <= gf_n:
            owner = at_x(-k)
            if k > 0:
                gather_f[g, k - 1].wait_recv()
            if k < gf_n:
                view = hid.at[c, g * nx + owner]
                i = g * (nx - 1) + k
                copy = remote(view, view, a_ss.at[i], a_rs.at[i], dev_x(1))
                copy.start()
                gather_f[g, k] = copy
                sends.append(copy)
            if k > 0:
                give(g, owner, k)
        if k <= gb_n:
            owner = at_x(k)
            if k > 0:
                gather_b[g, k - 1].wait_recv()
            if k < gb_n:
                view = hid.at[c, g * nx + owner]
                i = g * (nx - 1) + gf_n + k
                copy = remote(view, view, a_ss.at[i], a_rs.at[i], dev_x(-1))
                copy.start()
                gather_b[g, k] = copy
                sends.append(copy)
            if k > 0:
                give(g, owner, gf_n + k)
        if k == 0:
            give(g, x, 0)

    returns = []

    def second_product(g):
        if g == 0:
            loads[5].wait()
        for n in range(nx):
            given[g, n].wait_recv()
        h0 = hid[0, g * nx : (g + 1) * nx].reshape(nx * CH, half)
        h1 = hid[1, g * nx : (g + 1) * nx].reshape(nx * CH, half)
        value = jnp.dot(h0, wd[0:half, :], preferred_element_type=F32)
        value += jnp.dot(h1, wd[half : 2 * half, :], preferred_element_type=F32)
        osb[g * nx : (g + 1) * nx] = value.reshape(nx, CH, feat)
        at = g * nx
        while at < (g + 1) * nx:
            p = at // per
            end = min((p + 1) * per, (g + 1) * nx)
            lo, hi_ = at - p * per, end - p * per
            if p == 0:
                ret[z, lo:hi_] = osb[at:end]
            else:
                i = len(returns)
                copy = remote(
                    osb.at[at:end], ret.at[z, lo:hi_], o_ss.at[i], o_rs.at[i], dev_z(order[p])
                )
                copy.start()
                returns.append(copy)
                sends.append(copy)
            at = end

    stages = [lambda g: (first_product(g), reduce_step(g, 0))]
    for k in range(1, fwd_n):
        stages.append(functools.partial(lambda k, g: reduce_step(g, k), k))
    stages.append(finish)
    for k in range(1, max(gf_n, gb_n) + 1):
        stages.append(functools.partial(lambda k, g: gather_step(g, k), k))
    stages.append(second_product)
    for slot in range(len(stages) + lag * (groups - 1)):
        for g in range(groups):
            if 0 <= slot - lag * g < len(stages):
                stages[slot - lag * g](g)

    for copy in returns:
        copy.wait_recv()
    rows = ret[...].reshape(ne * cap, feat)
    total = lax.dot_general(
        comb[...], rows, (((0,), (0,)), ((), ())), preferred_element_type=F32, precision=lax.Precision.HIGHEST
    )
    piece = tokens_n // nf
    mix[...] = total.reshape(nf, piece, feat)
    first_y, second_y = [], []
    for k in range(1, nf):
        copy = remote(mix.at[(y + k) % nf], yrecv.at[k], y1_ss.at[k], y1_rs.at[k], dev_y(k))
        copy.start()
        first_y.append(copy)
        sends.append(copy)
    value = mix[y]
    for k in range(1, nf):
        first_y[k - 1].wait_recv()
        value = value + yrecv[k]
    yown[...] = value.astype(BF)
    res[y] = yown[...]
    for k in range(1, nf):
        copy = remote(yown, res.at[y], y2_ss.at[k], y2_rs.at[k], dev_y(k))
        copy.start()
        second_y.append(copy)
        sends.append(copy)
    for copy in second_y:
        copy.wait_recv()
    out_ref[...] = res[...].reshape(tokens_n, feat)
    for copy in sends:
        copy.wait_send()


def solution(mesh):
    ne, nf, nt = mesh.shape["expert"], mesh.shape["fsdp"], mesh.shape["tensor"]
    nx = nt // 2

    def body(tokens, expert_ids, gate_probs, w_gate, w_up, w_down):
        rows, feat = tokens.shape
        width = w_gate.shape[2]
        half = width // 2
        cap = 3 * rows // ne
        per = cap // CH
        chunks = ne * per
        groups = chunks // nx
        fwd_n, bwd_n = nx // 2, nx - 1 - nx // 2
        cfg = dict(ne=ne, nf=nf, nx=nx, cap=cap, half=half, lag=1, tile=256 if width % 256 == 0 else 128)
        any_ = pl.BlockSpec(memory_space=pl.ANY)
        dma = pltpu.SemaphoreType.DMA
        segments = chunks
        call = pl.pallas_call(
            functools.partial(kernel, cfg),
            out_shape=jax.ShapeDtypeStruct((rows, feat), BF),
            in_specs=[any_] * 6,
            out_specs=pl.BlockSpec(memory_space=pltpu.VMEM),
            scratch_shapes=[
                pltpu.VMEM((rows, feat), BF),
                pltpu.VMEM((2, rows), jnp.int32),
                pltpu.VMEM((2, rows), F32),
                pltpu.VMEM((2, feat, width), BF),
                pltpu.VMEM((width, feat), BF),
                pltpu.VMEM((ne, per, CH, feat), BF),
                pltpu.VMEM((ne * cap, rows), F32),
                pltpu.VMEM((2, chunks, CH, feat), BF),
                pltpu.VMEM((chunks, CH, width), F32),
                pltpu.VMEM((groups, max(fwd_n - 1, 1), CH, width), BF),
                pltpu.VMEM((groups, max(bwd_n, 1), CH, width), BF),
                pltpu.VMEM((groups, CH, width), F32),
                pltpu.VMEM((groups, max(fwd_n - 1, 1), CH, width), BF),
                pltpu.VMEM((groups, max(bwd_n, 1), CH, width), BF),
                pltpu.VMEM((groups, CH, width), F32),
                pltpu.VMEM((2, chunks, CH, half), BF),
                pltpu.VMEM((chunks, CH, feat), F32),
                pltpu.VMEM((ne, per, CH, feat), F32),
                pltpu.VMEM((nf, rows // nf, feat), F32),
                pltpu.VMEM((nf, rows // nf, feat), F32),
                pltpu.VMEM((rows // nf, feat), BF),
                pltpu.VMEM((nf, rows // nf, feat), BF),
                dma((6,)),
                dma((2,)), dma((2,)),
                dma((ne,)), dma((ne,)),
                dma((ne,)), dma((ne,)),
                dma((groups * (nx - 1),)), dma((groups * (nx - 1),)),
                dma((groups * (nx - 1),)), dma((groups * (nx - 1),)),
                dma((groups * nx,)), dma((groups * nx,)),
                dma((segments,)), dma((segments,)),
                dma((nf,)), dma((nf,)),
                dma((nf,)), dma((nf,)),
            ],
            compiler_params=pltpu.CompilerParams(
                collective_id=0, has_side_effects=True, vmem_limit_bytes=60 << 20
            ),
        )
        return call(tokens, expert_ids.T, gate_probs.T, w_gate[0], w_up[0], w_down[0])

    return jax.shard_map(
        body,
        mesh=mesh,
        in_specs=(
            P("expert", "tensor"),
            P("expert", None),
            P("expert", None),
            P("expert", "tensor", "fsdp"),
            P("expert", "tensor", "fsdp"),
            P("expert", "fsdp", "tensor"),
        ),
        out_specs=P("expert", "tensor"),
        check_vma=False,
    )
```

time: 270 us -> 89.9 us (0.33)
  waiting for transfers between devices: 207 us -> 0 us
  Pallas kernels: 0 us -> 88.2 us
  blocking collectives: 27 us -> 0 us
  between operations: 13.2 us -> 0.01 us
  starting transfers between devices: 8.2 us -> 0 us
  other arithmetic: 6.51 us -> 0 us
  matrix products: 3.91 us -> 0 us
    pallas_call x0 -> x1, Pallas kernels: none -> 88.2 us  [body(): call(tokens, expert_ids.T, gate_probs.T, w_gate[0], w_up[0], w_down[0])]
    psum x1 -> x0, waiting for transfers between devices: 83.9 us -> none  [body(): expert_total = lax.psum(partial_value, 'fsdp')]
    reduce_scatter x1 -> x0, waiting for transfers between devices: 63.3 us -> none  [body(): lax.psum_scatter(jnp.concatenate([gate_term, up_term], axis=1), 'tensor',...]
    all_gather x1 -> x0, waiting for transfers between devices: 48.6 us -> none  [body(): lax.all_gather(hidden_share, 'tensor', axis=0, tiled=True)]
    all_to_all x1 -> x0, blocking collectives: 27 us -> none  [body(): lax.all_to_all(outgoing, 'expert', split_axis=0, concat_axis=0, tiled=True)]
    all_to_all x1 -> x0, waiting for transfers between devices: 11.5 us -> none  [body(): lax.all_to_all(expert_total.reshape(experts, capacity, -1), 'expert', spl...]
    all_to_all x1 -> x0, starting transfers between devices: 8.11 us -> none  [body(): lax.all_to_all(expert_total.reshape(experts, capacity, -1), 'expert', spl...]
    dot_general x4 -> x0, matrix products: 3.91 us -> none  [the longest x1 2.64 us: body(): jnp.dot(lax.all_gather(hidden_share, 'tensor', axis=0, tiled=True), down_...]
  transfers between devices with their start and end apart: 4 -> 0, of which waited for: 4 -> 0; matrix products, arithmetic and copies ran while one was open for 0% -> 0% of each run, Pallas kernels for 0% -> 0%
where the time goes in v1:
time: 89.9 us; the launch traced here: 89.7 us
  Pallas kernels  88.2 us (98%)
  local copies, waits for them, and re-layouts  1.47 us (2%)
    pallas_call x1, Pallas kernels, body(): call(tokens, expert_ids.T, gate_probs.T, w_gate[0], w_up[0], w_down[0])  88.2 us

profile of v1, /device:TPU:2, one launch (start us, length us, event | category | flops | bytes accessed | tf_op | source)
XLA Modules:
  0.0 89.7 jit_solution(7716895760419774446)
XLA Ops:
  0.0 88.2 %shard_map.64 = bf16[128,256]{1,0:T(8,128)(2,1)} custom-call(bf16[128,256]{1,0:T(8,128)(2,1)} %tok_hbm.1, s32[2,128]{1,0:T(2,128)} %bitcast.8, f32[2,128]{1,0:T(2,128)} %bitcast.9, bf16[256,1792]{1,0:T(8,128)(2,1)} %bitcast.5, bf16[256,1792]{1,0:T(8,128)(2,1)} %bitcast.6, bf16[1792,256]{1,0:T(8,128)(2,1)} %bitcast.7), custom_call_target="tpu_custom_call" | custom-call | tf_op jit(solution)/shard_map/pallas_call | solution.py:391
  88.2 1.5 %copy.8 = bf16[128,256]{1,0:T(8,128)(2,1)} copy(bf16[128,256]{1,0:T(8,128)(2,1)} %shard_map.64) | data formatting | bytes 131072

commit v2 on v1

v2 whole, which is shorter than its diff:
```python
import functools

import jax
import jax.numpy as jnp
from jax import lax
from jax.experimental import pallas as pl
from jax.experimental.pallas import tpu as pltpu
from jax.sharding import PartitionSpec as P

MESH = pl.DeviceIdType.MESH
CH = 16
BF = jnp.bfloat16
F32 = jnp.float32


def kernel(
    cfg,
    tok_hbm, ids_hbm, prob_hbm, wg_hbm, wu_hbm, wd_hbm, out_ref,
    tok, ids, prob, wgu, wd, outg, comb, xs, part, sb, rb, hid, osb, ret, yrecv, fin,
    ld_sem, w_ss, w_rs, d_ss, d_rs, f_ss, f_rs, r_ss, r_rs, a_ss, a_rs, h_ss, h_rs, y1_ss, y1_rs, y2_ss, y2_rs,
):
    ne, nf, nx, cap = cfg["ne"], cfg["nf"], cfg["nx"], cfg["cap"]
    half, lag = cfg["half"], cfg["lag"]
    per = cap // CH
    groups = ne * per // nx
    rows_y = nx * CH // nf
    in_block = cap // rows_y
    routes = []
    for way, reach in ((1, nx // 2), (-1, nx - 1 - nx // 2)):
        for d in range(reach, 1, -2):
            routes += [(way, d, "leaf"), (way, d - 1, "relay")]
        if reach % 2:
            routes.append((way, 1, "alone"))
    tokens_n = tok.shape[0]
    feat = tok.shape[1]

    z, y, t = lax.axis_index("expert"), lax.axis_index("fsdp"), lax.axis_index("tensor")
    x, c = t // 2, t % 2
    other = 1 - c
    sgn = 1 - 2 * c
    partner = (z, y, x * 2 + other)

    def at_x(k):
        return (x + sgn * k + 2 * nx) % nx

    def dev_x(k):
        return (z, y, at_x(k) * 2 + c)

    def dev_z(k):
        return ((z + k + ne) % ne, y, t)

    def dev_y(k):
        return (z, (y + k + nf) % nf, t)

    class Remote:
        def __init__(self, src, dst, ss, rs, dev):
            self.copy = pltpu.make_async_remote_copy(
                src_ref=src, dst_ref=dst, send_sem=ss, recv_sem=rs, device_id=dev, device_id_type=MESH
            )
            self.start, self.wait_send, self.waited = self.copy.start, self.copy.wait_send, False

        def wait_recv(self):
            if not self.waited:
                self.copy.wait_recv()
            self.waited = True

    remote = Remote
    sends = []

    mine = pl.ds(pl.multiple_of(c * half, 128), half)
    theirs = pl.ds(pl.multiple_of(other * half, 128), half)
    loads = [
        pltpu.make_async_copy(ids_hbm, ids, ld_sem.at[0]),
        pltpu.make_async_copy(prob_hbm, prob, ld_sem.at[1]),
        pltpu.make_async_copy(tok_hbm, tok, ld_sem.at[2]),
        pltpu.make_async_copy(wg_hbm.at[:, mine], wgu.at[c, :, 0:half], ld_sem.at[3]),
        pltpu.make_async_copy(wu_hbm.at[:, mine], wgu.at[c, :, half : 2 * half], ld_sem.at[4]),
        pltpu.make_async_copy(wd_hbm, wd, ld_sem.at[5]),
    ]
    for copy in loads:
        copy.start()

    barrier = pltpu.get_barrier_semaphore()
    peers = [partner]
    offsets = {way * d % nx for way, d, kind in routes if kind != "leaf"} | {way % nx for way, d, kind in routes}
    peers += [dev_x(k) for k in sorted(offsets | {-k % nx for k in offsets})]
    peers += [dev_z(k) for k in range(1, ne)]
    peers += [dev_y(k) for k in range(1, nf)]
    for peer in peers:
        pl.semaphore_signal(barrier, inc=1, device_id=peer, device_id_type=MESH)

    loads[0].wait()
    loads[1].wait()
    expert_row = lax.broadcasted_iota(jnp.int32, (ne, tokens_n), 0)
    first = expert_row == ids[0:1, :]
    second = expert_row == ids[1:2, :]
    named = jnp.where(first, 1.0, 0.0) + jnp.where(second, 1.0, 0.0)
    weight = jnp.where(first, prob[0:1, :], 0.0) + jnp.where(second, prob[1:2, :], 0.0)
    earlier = jnp.where(
        lax.broadcasted_iota(jnp.int32, (tokens_n, tokens_n), 0)
        < lax.broadcasted_iota(jnp.int32, (tokens_n, tokens_n), 1),
        1.0,
        0.0,
    ).astype(BF)
    rank = jnp.dot(named.astype(BF), earlier, preferred_element_type=F32)
    rank = jnp.where(named > 0.5, rank, -1.0)
    slot_row = lax.broadcasted_iota(jnp.int32, (cap, tokens_n), 0).astype(F32)
    hi = weight.astype(BF).astype(F32)
    mid = (weight - hi).astype(BF).astype(F32)
    low = weight - hi - mid
    loads[2].wait()
    for e in range(ne):
        chosen = slot_row == rank[e : e + 1, :]
        rows = jnp.dot(jnp.where(chosen, 1.0, 0.0).astype(BF), tok[...], preferred_element_type=F32)
        outg[e] = rows.astype(BF).reshape(per, CH, feat)
        for i, term in enumerate((hi, mid, low)):
            comb[i, e * cap : (e + 1) * cap, :] = jnp.where(chosen, term[e : e + 1, :], 0.0).astype(BF)

    pl.semaphore_wait(barrier, len(peers))

    swaps = [
        remote(wg_hbm.at[:, theirs], wgu.at[c, :, 0:half], w_ss.at[0], w_rs.at[0], partner),
        remote(wu_hbm.at[:, theirs], wgu.at[c, :, half : 2 * half], w_ss.at[1], w_rs.at[1], partner),
    ]
    for copy in swaps:
        copy.start()
        sends.append(copy)

    xs[c, 0:per] = outg[z]
    dispatch = [None]
    for p in range(1, ne):
        copy = remote(
            outg.at[(z - p + ne) % ne], xs.at[c, p * per : (p + 1) * per], d_ss.at[p], d_rs.at[p], dev_z(-p)
        )
        copy.start()
        dispatch.append(copy)
        sends.append(copy)

    handed = {}

    def hand(p):
        if p in handed:
            return
        if p > 0:
            dispatch[p].wait_recv()
        view = xs.at[c, p * per : (p + 1) * per]
        copy = remote(view, view, f_ss.at[p], f_rs.at[p], partner)
        copy.start()
        handed[p] = copy
        sends.append(copy)

    def blocks_of(g):
        return range(g * nx // per, ((g + 1) * nx - 1) // per + 1)

    taken = set()
    loaded = []

    def first_product(g):
        for p in blocks_of(g):
            hand(p)
        if not loaded:
            for copy in (loads[3], loads[4]):
                copy.wait()
            for copy in swaps:
                copy.wait_recv()
            loaded.append(1)
        for p in blocks_of(g):
            if p not in taken:
                handed[p].wait_recv()
                taken.add(p)
        a0 = xs[0, g * nx : (g + 1) * nx].reshape(nx * CH, feat)
        a1 = xs[1, g * nx : (g + 1) * nx].reshape(nx * CH, feat)
        tile = cfg["tile"]
        for n in range(2 * half // tile):
            cols = slice(n * tile, (n + 1) * tile)
            acc = jnp.dot(a0, wgu[0, :, cols], preferred_element_type=F32)
            acc += jnp.dot(a1, wgu[1, :, cols], preferred_element_type=F32)
            part[g * nx : (g + 1) * nx, :, cols] = acc.reshape(nx, CH, tile)

    got = {}

    def leaf_sends(g):
        for i, (way, d, kind) in enumerate(routes):
            if kind == "relay":
                continue
            sb[g, i] = part[g * nx + at_x(way * d)].astype(BF)
            j = g * (nx - 1) + i
            copy = remote(sb.at[g, i], rb.at[g, i], r_ss.at[j], r_rs.at[j], dev_x(way))
            copy.start()
            got[g, i] = copy
            sends.append(copy)

    def relay_sends(g):
        for i, (way, d, kind) in enumerate(routes):
            if kind != "relay":
                continue
            k = routes.index((way, d + 1, "leaf"))
            value = part[g * nx + at_x(way * d)]
            got[g, k].wait_recv()
            sb[g, i] = (value + rb[g, k].astype(F32)).astype(BF)
            j = g * (nx - 1) + i
            copy = remote(sb.at[g, i], rb.at[g, i], r_ss.at[j], r_rs.at[j], dev_x(way * d))
            copy.start()
            got[g, i] = copy
            sends.append(copy)

    given = {}

    def give(g, owner, n):
        view = hid.at[c, g * nx + owner]
        i = g * nx + n
        copy = remote(view, view, h_ss.at[i], h_rs.at[i], partner)
        copy.start()
        given[g, n] = copy
        sends.append(copy)

    def finish(g):
        value = part[g * nx + x]
        for i, (way, d, kind) in enumerate(routes):
            if kind != "leaf":
                got[g, i].wait_recv()
                value = value + rb[g, i].astype(F32)
        gate, up = value[:, :half], value[:, half:]
        hid[c, g * nx + x] = (gate / (1.0 + jnp.exp(-gate)) * up).astype(BF)
        for i, (way, d, kind) in enumerate(routes):
            if kind != "leaf":
                spread(g, i, x, way * d)
        give(g, x, nx - 1)

    shared = {}

    def spread(g, i, owner, to):
        view = hid.at[c, g * nx + owner]
        j = g * (nx - 1) + i
        copy = remote(view, view, a_ss.at[j], a_rs.at[j], dev_x(to))
        copy.start()
        shared[g, i] = copy
        sends.append(copy)

    def relay_hidden(g):
        for i, (way, d, kind) in enumerate(routes):
            if kind == "leaf":
                continue
            shared[g, i].wait_recv()
            owner = at_x(-way * d)
            if kind == "relay":
                spread(g, routes.index((way, d + 1, "leaf")), owner, way)
            give(g, owner, i)

    def collect_hidden(g):
        for i, (way, d, kind) in enumerate(routes):
            if kind == "leaf":
                shared[g, i].wait_recv()
                give(g, at_x(-way * d), i)

    summed, cast = {}, {}

    def second_product(g):
        if g == 0:
            loads[5].wait()
        for n in range(nx):
            given[g, n].wait_recv()
        h0 = hid[0, g * nx : (g + 1) * nx].reshape(nx * CH, half)
        h1 = hid[1, g * nx : (g + 1) * nx].reshape(nx * CH, half)
        value = jnp.dot(h0, wd[0:half, :], preferred_element_type=F32)
        value += jnp.dot(h1, wd[half : 2 * half, :], preferred_element_type=F32)
        osb[g] = value.reshape(nf, rows_y, feat)
        for k in range(1, nf):
            i = g * nf + k
            copy = remote(osb.at[g, (y + k) % nf], yrecv.at[g, k], y1_ss.at[i], y1_rs.at[i], dev_y(k))
            copy.start()
            summed[g, k] = copy
            sends.append(copy)

    def send_back(g):
        value = osb[g, y]
        for k in range(1, nf):
            summed[g, k].wait_recv()
            value = value + yrecv[g, k]
        fin[g] = value.astype(BF)
        q = g * nf + y
        home = q // in_block
        place = ret.at[z, q % in_block]
        to_z = (z + home) % ne
        for k in range(nf):
            i = g * nf + k
            copy = remote(fin.at[g], place, y2_ss.at[i], y2_rs.at[q], (to_z, (y + k) % nf, t))
            if k == 0 and g * nf < in_block:
                kept = q < in_block

                @pl.when(kept)
                def _():
                    ret[z, q % in_block] = fin[g]

                @pl.when(jnp.logical_not(kept))
                def _():
                    copy.start()

                own_sends.append((kept, copy))
            else:
                copy.start()
                sends.append(copy)

    own_sends = []
    stages = [
        lambda g: (first_product(g), leaf_sends(g)), relay_sends, finish, relay_hidden, collect_hidden, second_product, send_back,
    ]
    for slot in range(len(stages) + lag * (groups - 1)):
        for g in range(groups):
            if 0 <= slot - lag * g < len(stages):
                stages[slot - lag * g](g)

    for q in range(groups * nf):
        copy = remote(fin.at[0], ret.at[0, 0], y2_ss.at[0], y2_rs.at[q], partner)
        if q < in_block:

            @pl.when(y != q % nf)
            def _():
                copy.wait_recv()

        else:
            copy.wait_recv()
    back = ret[...].reshape(ne * cap, feat)
    total = jnp.zeros((tokens_n, feat), F32)
    for i in range(3):
        total += lax.dot_general(comb[i], back, (((0,), (0,)), ((), ())), preferred_element_type=F32)
    out_ref[...] = total.astype(BF)
    for copy in sends:
        copy.wait_send()
    for kept, copy in own_sends:

        @pl.when(jnp.logical_not(kept))
        def _():
            copy.wait_send()


def solution(mesh):
    ne, nf, nt = mesh.shape["expert"], mesh.shape["fsdp"], mesh.shape["tensor"]
    nx = nt // 2

    def body(tokens, expert_ids, gate_probs, w_gate, w_up, w_down):
        rows, feat = tokens.shape
        width = w_gate.shape[2]
        half = width // 2
        cap = 3 * rows // ne
        per = cap // CH
        chunks = ne * per
        groups = chunks // nx
        cfg = dict(ne=ne, nf=nf, nx=nx, cap=cap, half=half, lag=0, tile=256 if width % 256 == 0 else 128)
        any_ = pl.BlockSpec(memory_space=pl.ANY)
        dma = pltpu.SemaphoreType.DMA
        piece = nx * CH // nf
        call = pl.pallas_call(
            functools.partial(kernel, cfg),
            out_shape=jax.ShapeDtypeStruct((rows, feat), BF),
            in_specs=[any_] * 6,
            out_specs=pl.BlockSpec(memory_space=pltpu.VMEM),
            scratch_shapes=[
                pltpu.VMEM((rows, feat), BF),
                pltpu.VMEM((2, rows), jnp.int32),
                pltpu.VMEM((2, rows), F32),
                pltpu.VMEM((2, feat, width), BF),
                pltpu.VMEM((width, feat), BF),
                pltpu.VMEM((ne, per, CH, feat), BF),
                pltpu.VMEM((3, ne * cap, rows), BF),
                pltpu.VMEM((2, chunks, CH, feat), BF),
                pltpu.VMEM((chunks, CH, width), F32),
                pltpu.VMEM((groups, nx - 1, CH, width), BF),
                pltpu.VMEM((groups, nx - 1, CH, width), BF),
                pltpu.VMEM((2, chunks, CH, half), BF),
                pltpu.VMEM((groups, nf, piece, feat), F32),
                pltpu.VMEM((ne, cap // piece, piece, feat), BF),
                pltpu.VMEM((groups, nf, piece, feat), F32),
                pltpu.VMEM((groups, piece, feat), BF),
                dma((6,)),
                dma((2,)), dma((2,)),
                dma((ne,)), dma((ne,)),
                dma((ne,)), dma((ne,)),
                dma((groups * (nx - 1),)), dma((groups * (nx - 1),)),
                dma((groups * (nx - 1),)), dma((groups * (nx - 1),)),
                dma((groups * nx,)), dma((groups * nx,)),
                dma((groups * nf,)), dma((groups * nf,)),
                dma((groups * nf,)), dma((groups * nf,)),
            ],
            compiler_params=pltpu.CompilerParams(
                collective_id=0, has_side_effects=True, vmem_limit_bytes=60 << 20
            ),
        )
        return call(tokens, expert_ids.T, gate_probs.T, w_gate[0], w_up[0], w_down[0])

    return jax.shard_map(
        body,
        mesh=mesh,
        in_specs=(
            P("expert", "tensor"),
            P("expert", None),
            P("expert", None),
            P("expert", "tensor", "fsdp"),
            P("expert", "tensor", "fsdp"),
            P("expert", "fsdp", "tensor"),
        ),
        out_specs=P("expert", "tensor"),
        check_vma=False,
    )
```

time: 89.9 us -> 82.8 us (0.921)
  the two profiles are of different devices: /device:TPU:2 before, /device:TPU:16 now
where the time goes in v2:
time: 82.8 us; the launch traced here: 82.6 us
  Pallas kernels  81.1 us (98%)
  local copies, waits for them, and re-layouts  1.47 us (2%)
    pallas_call x1, Pallas kernels, body(): call(tokens, expert_ids.T, gate_probs.T, w_gate[0], w_up[0], w_down[0])  81.1 us

profile of v2, /device:TPU:16, one launch (start us, length us, event | category | flops | bytes accessed | tf_op | source)
XLA Modules:
  0.0 82.6 jit_solution(7788395040562387643)
XLA Ops:
  0.0 81.1 %shard_map.64 = bf16[128,256]{1,0:T(8,128)(2,1)} custom-call(bf16[128,256]{1,0:T(8,128)(2,1)} %tok_hbm.1, s32[2,128]{1,0:T(2,128)} %bitcast.8, f32[2,128]{1,0:T(2,128)} %bitcast.9, bf16[256,1792]{1,0:T(8,128)(2,1)} %bitcast.5, bf16[256,1792]{1,0:T(8,128)(2,1)} %bitcast.6, bf16[1792,256]{1,0:T(8,128)(2,1)} %bitcast.7), custom_call_target="tpu_custom_call" | custom-call | tf_op jit(solution)/shard_map/pallas_call | solution.py:389
  81.1 1.5 %copy.8 = bf16[128,256]{1,0:T(8,128)(2,1)} copy(bf16[128,256]{1,0:T(8,128)(2,1)} %shard_map.64) | data formatting | bytes 131072

commit v3 on v2

--- a/solution.py
+++ b/solution.py
@@ -20,7 +20,7 @@
     ld_sem, w_ss, w_rs, d_ss, d_rs, f_ss, f_rs, r_ss, r_rs, a_ss, a_rs, h_ss, h_rs, y1_ss, y1_rs, y2_ss, y2_rs,
 ):
     ne, nf, nx, cap = cfg["ne"], cfg["nf"], cfg["nx"], cfg["cap"]
-    half, lag = cfg["half"], cfg["lag"]
+    half = cfg["half"]
     per = cap // CH
     groups = ne * per // nx
     rows_y = nx * CH // nf
@@ -179,9 +179,9 @@
 
     got = {}
 
-    def leaf_sends(g):
-        for i, (way, d, kind) in enumerate(routes):
-            if kind == "relay":
+    def send_own(g, only):
+        for i, (way, d, kind) in enumerate(routes):
+            if kind != only:
                 continue
             sb[g, i] = part[g * nx + at_x(way * d)].astype(BF)
             j = g * (nx - 1) + i
@@ -203,6 +203,7 @@
             copy.start()
             got[g, i] = copy
             sends.append(copy)
+        send_own(g, "alone")
 
     given = {}
 
@@ -303,12 +304,11 @@
 
     own_sends = []
     stages = [
-        lambda g: (first_product(g), leaf_sends(g)), relay_sends, finish, relay_hidden, collect_hidden, second_product, send_back,
+        lambda g: (first_product(g), send_own(g, "leaf")), relay_sends, finish, relay_hidden, collect_hidden, second_product, send_back,
     ]
-    for slot in range(len(stages) + lag * (groups - 1)):
-        for g in range(groups):
-            if 0 <= slot - lag * g < len(stages):
-                stages[slot - lag * g](g)
+    start, pace = (0, 3, 5, 8, 11, 14, 18), (1, 1.6, 2, 2, 2, 1.6, 1)
+    for _, n, g in sorted((start[n] + pace[n] * g, n, g) for n in range(len(stages)) for g in range(groups)):
+        stages[n](g)
 
     for q in range(groups * nf):
         copy = remote(fin.at[0], ret.at[0, 0], y2_ss.at[0], y2_rs.at[q], partner)
@@ -346,7 +346,7 @@
         per = cap // CH
         chunks = ne * per
         groups = chunks // nx
-        cfg = dict(ne=ne, nf=nf, nx=nx, cap=cap, half=half, lag=0, tile=256 if width % 256 == 0 else 128)
+        cfg = dict(ne=ne, nf=nf, nx=nx, cap=cap, half=half, tile=256 if width % 256 == 0 else 128)
         any_ = pl.BlockSpec(memory_space=pl.ANY)
         dma = pltpu.SemaphoreType.DMA
         piece = nx * CH // nf

time: 82.8 us -> 80.7 us (0.975)
  the two profiles are of different devices: /device:TPU:16 before, /device:TPU:2 now
where the time goes in v3:
time: 80.7 us; the launch traced here: 80.5 us
  Pallas kernels  79.1 us (98%)
  local copies, waits for them, and re-layouts  1.47 us (2%)
    pallas_call x1, Pallas kernels, body(): call(tokens, expert_ids.T, gate_probs.T, w_gate[0], w_up[0], w_down[0])  79.1 us

profile of v3, /device:TPU:2, one launch (start us, length us, event | category | flops | bytes accessed | tf_op | source)
XLA Modules:
  0.0 80.5 jit_solution(8260030322784493450)
XLA Ops:
  0.0 79.1 %shard_map.64 = bf16[128,256]{1,0:T(8,128)(2,1)} custom-call(bf16[128,256]{1,0:T(8,128)(2,1)} %tok_hbm.1, s32[2,128]{1,0:T(2,128)} %bitcast.8, f32[2,128]{1,0:T(2,128)} %bitcast.9, bf16[256,1792]{1,0:T(8,128)(2,1)} %bitcast.5, bf16[256,1792]{1,0:T(8,128)(2,1)} %bitcast.6, bf16[1792,256]{1,0:T(8,128)(2,1)} %bitcast.7), custom_call_target="tpu_custom_call" | custom-call | tf_op jit(solution)/shard_map/pallas_call | solution.py:389
  79.1 1.5 %copy.8 = bf16[128,256]{1,0:T(8,128)(2,1)} copy(bf16[128,256]{1,0:T(8,128)(2,1)} %shard_map.64) | data formatting | bytes 131072

commit v4 on v3

--- a/solution.py
+++ b/solution.py
@@ -156,7 +156,7 @@
     loaded = []
 
     def first_product(g):
-        for p in blocks_of(g):
+        for p in blocks_of(g) if g == 0 else range(ne):
             hand(p)
         if not loaded:
             for copy in (loads[3], loads[4]):

time: 80.7 us -> 80.4 us (level)
  the two profiles are of different devices: /device:TPU:2 before, /device:TPU:32 now
where the time goes in v4:
time: 80.4 us; the launch traced here: 80.2 us
  Pallas kernels  78.7 us (98%)
  local copies, waits for them, and re-layouts  1.47 us (2%)
    pallas_call x1, Pallas kernels, body(): call(tokens, expert_ids.T, gate_probs.T, w_gate[0], w_up[0], w_down[0])  78.7 us

profile of v4, /device:TPU:32, one launch (start us, length us, event | category | flops | bytes accessed | tf_op | source)
XLA Modules:
  0.0 80.2 jit_solution(3209185043471923729)
XLA Ops:
  0.0 78.7 %shard_map.64 = bf16[128,256]{1,0:T(8,128)(2,1)} custom-call(bf16[128,256]{1,0:T(8,128)(2,1)} %tok_hbm.1, s32[2,128]{1,0:T(2,128)} %bitcast.8, f32[2,128]{1,0:T(2,128)} %bitcast.9, bf16[256,1792]{1,0:T(8,128)(2,1)} %bitcast.5, bf16[256,1792]{1,0:T(8,128)(2,1)} %bitcast.6, bf16[1792,256]{1,0:T(8,128)(2,1)} %bitcast.7), custom_call_target="tpu_custom_call" | custom-call | tf_op jit(solution)/shard_map/pallas_call | solution.py:389
  78.7 1.5 %copy.8 = bf16[128,256]{1,0:T(8,128)(2,1)} copy(bf16[128,256]{1,0:T(8,128)(2,1)} %shard_map.64) | data formatting | bytes 131072
